TPU v7x, 32 devices: a whole 2x2x4 slice. The times are simulated.
32 devices in a mesh: segment: 4 (over y, x), seq: 8 (over z, core).
Axes of the slice: x: 2, y: 2, z: 4, core: 2. Of those that a mesh axis runs over, the one named last changes fastest.
Arguments:
- hidden: bfloat16 [4, 8192, 8192], P('segment', 'seq'), may hold values from -6 to 6
- span_lengths: int32 [4, 64], replicated, may hold values from 1 to 512, 8192 in all within a row
- section_of: int32 [4, 64], replicated, may hold values from 0 to 31
- section_live: int32 [32], P('seq'), may hold values 0 or 1
- w_in: bfloat16 [8192, 2048], P('seq'), may hold values from -0.5 to 0.5
- norm_gain: float32 [2048], replicated, may hold values from 0.5 to 1.5
- w_query: bfloat16 [2048, 2048], P(None, 'segment'), may hold values from -0.125 to 0.125
- w_key: bfloat16 [2048, 2048], P(None, 'segment'), may hold values from -0.125 to 0.125
- w_value: bfloat16 [2048, 2048], P(None, 'segment'), may hold values from -0.125 to 0.125
- w_out: bfloat16 [2048, 2048], P('segment'), may hold values from -0.125 to 0.125
Outputs:
- section_out: bfloat16 [32, 2048], P('seq')
All inputs are finite; a program needn't handle non-finite values. No bound on the sum of `section_live` on one device may be relied on, other than what follows from the above.
Results may differ from a plain program's by a relative error of at most 0.007.
Values may be sent and summed in bfloat16 or wider, within the bound.
A program may use at most 128 MiB of HBM per device.

v0:
```python
import jax
import jax.numpy as jnp
from jax import lax
from jax.sharding import PartitionSpec as P

HEAD_DIM = 128


def shards(
    hidden, span_lengths, section_of, section_live, w_in, norm_gain, w_query, w_key, w_value, w_out
):
    tokens = hidden[0]
    seq_count = lax.axis_size("seq")
    seq_index = lax.axis_index("seq")
    segment_index = lax.axis_index("segment")
    tok_count = tokens.shape[0]
    lengths = lax.dynamic_index_in_dim(span_lengths, segment_index, 0, keepdims=False)
    span_ends = jnp.cumsum(lengths)
    span_starts = span_ends - lengths
    positions = seq_index * tok_count + jnp.arange(tok_count, dtype=jnp.int32)
    member = (
        (positions[None, :] >= span_starts[:, None]) & (positions[None, :] < span_ends[:, None])
    ).astype(jnp.bfloat16)
    partial_value = jnp.dot(member, tokens, preferred_element_type=jnp.float32)
    length_float = lengths.astype(jnp.float32)
    sections_here = section_live.shape[0]
    section_total = sections_here * seq_count
    section_ids = jnp.arange(section_total, dtype=jnp.int32)
    own_sections = seq_index * sections_here + jnp.arange(sections_here, dtype=jnp.int32)
    flat_sections = section_of.reshape(-1)
    count_all = jnp.sum(
        (section_ids[:, None] == flat_sections[None, :]).astype(jnp.float32), axis=1
    )
    doc_sections = lax.dynamic_index_in_dim(section_of, segment_index, 0, keepdims=False)
    weighted = partial_value / length_float[:, None]
    doc_onehot = (section_ids[:, None] == doc_sections[None, :]).astype(jnp.float32)
    section_part = jnp.dot(doc_onehot, weighted, precision=lax.Precision.HIGHEST)
    feature_block = lax.psum_scatter(section_part, "seq", scatter_dimension=1, tiled=True)
    doc_total = lax.psum(feature_block, "segment")
    pooled = (doc_total / jnp.maximum(count_all, 1.0)[:, None]).astype(jnp.bfloat16)
    projected = jnp.dot(pooled, w_in, preferred_element_type=jnp.float32)
    section_in = lax.psum_scatter(projected, "seq", scatter_dimension=0, tiled=True)
    scale = lax.rsqrt(jnp.mean(section_in * section_in, axis=1, keepdims=True) + 1e-05)
    normed = (section_in * scale * norm_gain[None, :]).astype(jnp.bfloat16)
    queries = jnp.dot(normed, w_query, preferred_element_type=jnp.float32).astype(jnp.bfloat16)
    keys_here = jnp.dot(normed, w_key, preferred_element_type=jnp.float32).astype(jnp.bfloat16)
    values_here = jnp.dot(normed, w_value, preferred_element_type=jnp.float32).astype(jnp.bfloat16)
    live_here = section_live.astype(jnp.bfloat16)
    keys_all, values_all, live_all = (
        lax.all_gather(keys_here, "seq", axis=0, tiled=True),
        lax.all_gather(values_here, "seq", axis=0, tiled=True),
        lax.all_gather(live_here, "seq", axis=0, tiled=True),
    )
    local_heads = queries.shape[1] // HEAD_DIM
    query_heads = queries.reshape(sections_here, local_heads, HEAD_DIM)
    key_heads = keys_all.reshape(section_total, local_heads, HEAD_DIM)
    value_heads = values_all.reshape(section_total, local_heads, HEAD_DIM)
    scores = jnp.einsum("qhd,khd->hqk", query_heads, key_heads, preferred_element_type=jnp.float32)
    scores = scores / jnp.sqrt(jnp.float32(HEAD_DIM))
    allowed = (live_all[None, :] > 0) | (section_ids[None, :] == own_sections[:, None])
    scores = jnp.where(allowed[None, :, :], scores, jnp.float32(-1e30))
    probs = jax.nn.softmax(scores, axis=-1).astype(jnp.bfloat16)
    attended = jnp.einsum(
        "hqk,khd->qhd", probs, value_heads, preferred_element_type=jnp.float32
    ).astype(jnp.bfloat16)
    attended = attended.reshape(sections_here, local_heads * HEAD_DIM)
    head_terms = jnp.dot(attended, w_out, preferred_element_type=jnp.float32)
    combined = lax.psum(head_terms, "segment")
    return (section_in + combined).astype(jnp.bfloat16)


def solution(mesh):
    in_specs = (
        P("segment", "seq", None),
        P(),
        P(),
        P("seq"),
        P("seq", None),
        P(),
        P(None, "segment"),
        P(None, "segment"),
        P(None, "segment"),
        P("segment", None),
    )
    out_specs = P("seq", None)
    return jax.shard_map(shards, mesh=mesh, in_specs=in_specs, out_specs=out_specs, check_vma=False)
```

profile of v0, /device:TPU:0, one launch (start us, length us, event | category | flops | bytes accessed | tf_op | source)
XLA Modules:
  0.0 217.7 jit_solution(10877947771555918930)
XLA Ops:
  6.5 0.0 copy-start
  6.5 0.0 reduce-scatter.2.cloned.1.call-start
  6.5 0.9 fusion.30
  7.4 0.1 copy.25
  7.5 0.1 reduce-window.7
  7.6 0.1 reduce
  7.7 0.7 bitcast_subtract_fusion
  8.4 8.8 %fusion.3 = f32[64,8192]{1,0:T(8,128)S(1)} fusion(bf16[1,1024,8192]{2,1,0:T(8,128)(2,1)} %param.10, f32[64]{0:T(128)S(1)} %get-tuple-element.6, s32[1024]{0:T(1024)S(1)} %iota_add_fusion, s32[64]{0:T(128)S(1)} %reduce, s32[64]{0:T(128)S(1)} %bitcast_subtract_fusion), kind=kOutput, calls=%fused_computation.3 | convolution fusion | flops 1074462720 | bytes 18879232 | tf_op jit(solution)/shard_map/dot_general | solution.py:24
  17.3 0.0 copy-start.2
  17.3 0.0 copy-start.4
  17.3 0.0 copy-start.3
  17.3 1.8 fusion.25
  19.1 0.0 reduce-scatter.2.cloned.1.call-update
  19.1 0.0 all-reduce.5.cloned.1.call-start
  19.2 0.0 copy-done.2
  19.2 0.1 eq.52
  19.3 0.0 copy-done.4
  19.3 0.0 copy-done.3
  19.3 0.7 fusion.31
  20.6 0.2 dynamic-update-slice
  20.9 18.2 %all-reduce = bf16[32]{0:T(256)(128)(2,1)S(1)} all-reduce(bf16[32]{0:T(256)(128)(2,1)S(1)} %dynamic-update-slice), channel_id=1, replica_groups=mesh['segment'=4,'seq'=8] {'seq'}, use_global_device_ids=true, to_apply=%add | all-reduce | flops 32 | bytes 128
  39.1 0.1 convert_reduce_fusion
  39.2 15.9 %reduce-scatter.2.cloned.1.call-done = f32[32,1024]{1,0:T(8,128)} async-done(((f32[32,8192]{1,0:T(8,128)}), f32[32,1024]{1,0:T(8,128)}) %reduce-scatter.2.cloned.1.call-update) | async-done | bytes 131088 | tf_op jit(solution)/shard_map/reduce_scatter | solution.py:38
  55.1 0.0 all-reduce.5.cloned.1.call-update
  55.1 0.0 all-reduce.7.cloned.1.call-start
  55.8 0.0 copy-start.1
  55.8 42.1 %all-reduce.5.cloned.1.call-done = f32[32,1024]{1,0:T(8,128)} async-done(((f32[32,1024]{1,0:T(8,128)}), f32[32,1024]{1,0:T(8,128)}) %all-reduce.5.cloned.1.call-update) | async-done | bytes 131088 | tf_op jit(solution)/shard_map/psum | solution.py:39
  97.9 3.8 %fusion.20 = f32[32,2048]{1,0:T(8,128)} fusion(bf16[1024,2048]{1,0:T(8,128)(2,1)} %param.14, f32[32,1024]{1,0:T(8,128)} %all-reduce.5.cloned.1.call-done, f32[32]{0:T(128)S(1)} %broadcast_maximum_fusion), kind=kOutput, calls=%fused_computation.24 | convolution fusion | flops 134283264 | bytes 4587648 | tf_op jit(solution)/shard_map/dot_general | solution.py:41
  101.7 0.0 all-reduce.7.cloned.1.call-update
  101.7 0.1 fusion.29
  101.8 55.5 %all-reduce.7.cloned.1.call-done = f32[32,2048]{1,0:T(8,128)} async-done(((f32[32,2048]{1,0:T(8,128)}), f32[32,2048]{1,0:T(8,128)}) %all-reduce.7.cloned.1.call-update) | async-done | bytes 262160
  157.3 1.0 multiply_reduce_fusion
  158.3 0.0 copy-done.1
  158.3 2.0 fusion.11
  160.3 14.1 %all-gather.1 = bf16[8,4,512]{2,1,0:T(4,128)(2,1)S(1)} all-gather(bf16[1,4,512]{2,1,0:T(4,128)(2,1)S(1)} %fusion.11), channel_id=1, replica_groups=mesh['segment'=4,'seq'=8] {'seq'}, dimensions={0}, use_global_device_ids=true | all-gather | bytes 36864 | tf_op jit(solution)/shard_map/all_gather | solution.py:50
  174.4 2.2 fusion.8
  176.6 0.2 fusion.32
  176.8 2.1 fusion.9
  178.8 14.1 %all-gather = bf16[8,4,512]{2,1,0:T(4,128)(2,1)S(1)} all-gather(bf16[1,4,512]{2,1,0:T(4,128)(2,1)S(1)} %fusion.9), channel_id=1, replica_groups=mesh['segment'=4,'seq'=8] {'seq'}, dimensions={0}, use_global_device_ids=true | all-gather | bytes 36864 | tf_op jit(solution)/shard_map/all_gather | solution.py:51
  192.9 0.0 copy-done
  193.0 0.5 fusion.13
  193.5 16.2 %psum.15 = f32[4,2048]{1,0:T(4,128)S(1)} all-reduce(f32[4,2048]{1,0:T(4,128)S(1)} %fusion.13), channel_id=1, replica_groups=mesh['segment'=4,'seq'=8] {'segment'}, use_global_device_ids=true, to_apply=%region_8.9 | all-reduce | flops 8192 | bytes 65536 | tf_op jit(solution)/shard_map/psum | solution.py:68
  209.7 1.5 add_convert_fusion
  (9 shorter events, 0.1 us)
Async XLA Ops:
  6.5 186.4 %copy-start = (bf16[512,2048]{1,0:T(8,128)(2,1)S(1)}, bf16[512,2048]{1,0:T(8,128)(2,1)}, u32[]{:S(2)}) copy-start(bf16[512,2048]{1,0:T(8,128)(2,1)} %param.19) | copy-start | bytes 6291460
  6.5 48.5 %reduce-scatter.2.cloned.1.call-start = ((), (), s32[]{:S(2)}) async-start(), calls=%async_computation.1 | async-start | bytes 1179648 | tf_op jit(solution)/shard_map/reduce_scatter | solution.py:38
  17.3 1.9 copy-start.2
  17.3 2.0 copy-start.4
  17.3 2.0 copy-start.3
  19.1 78.7 %all-reduce.5.cloned.1.call-start = ((), (), s32[]{:S(2)}) async-start(), calls=%async_computation.2 | async-start | bytes 262144 | tf_op jit(solution)/shard_map/psum | solution.py:39
  55.1 102.2 %all-reduce.7.cloned.1.call-start = ((), (), s32[]{:S(2)}) async-start(), calls=%async_computation.3 | async-start | bytes 524288
  55.8 102.5 %copy-start.1 = (f32[2048]{0:T(1024)S(1)}, f32[2048]{0:T(1024)}, u32[]{:S(2)}) copy-start(f32[2048]{0:T(1024)} %param.15) | copy-start | bytes 24580
Sparse Core Ops, SparseCore 0:
  19.3 35.7 reduce-scatter.1
  58.0 39.8 all-reduce.4
  101.9 55.4 all-reduce.6
where the time goes:
time: 218 us
  waiting for transfers between devices  113 us (52%)
  blocking collectives  62.6 us (29%)
  matrix products  21.3 us (10%)
  between operations  14.5 us (7%)
  other arithmetic  4.58 us (2%)
    unnamed x4, waiting for transfers between devices  55.5 us
    psum x1, waiting for transfers between devices, shards(): doc_total = lax.psum(feature_block, 'segment')  42.1 us
    unnamed x1, blocking collectives  18.2 us
    psum x1, blocking collectives, shards(): combined = lax.psum(head_terms, 'segment')  16.2 us
    reduce_scatter x1, waiting for transfers between devices, shards(): lax.psum_scatter(section_part, 'seq', scatter_dimension=1, tiled=True)  15.9 us
    all_gather x1, blocking collectives, shards(): lax.all_gather(keys_here, 'seq', axis=0, tiled=True)  14.1 us
    all_gather x1, blocking collectives, shards(): lax.all_gather(values_here, 'seq', axis=0, tiled=True)  14.1 us
    dot_general x1, matrix products, shards(): partial_value = jnp.dot(member, tokens, preferred_element_type=jnp.float32)  8.85 us
  transfers between devices with their start and end apart: 3, of which 3 were waited for; matrix products, arithmetic and copies ran while one was open for 1% of the time, Pallas kernels for 0%

commit v1 on v0

--- a/solution.py
+++ b/solution.py
@@ -36,7 +36,7 @@
     doc_onehot = (section_ids[:, None] == doc_sections[None, :]).astype(jnp.float32)
     section_part = jnp.dot(doc_onehot, weighted, precision=lax.Precision.HIGHEST)
     feature_block = lax.psum_scatter(section_part, "seq", scatter_dimension=1, tiled=True)
-    doc_total = lax.psum(feature_block, "segment")
+    doc_total = jnp.sum(lax.all_gather(feature_block, "segment"), axis=0)
     pooled = (doc_total / jnp.maximum(count_all, 1.0)[:, None]).astype(jnp.bfloat16)
     projected = jnp.dot(pooled, w_in, preferred_element_type=jnp.float32)
     section_in = lax.psum_scatter(projected, "seq", scatter_dimension=0, tiled=True)

time: 218 us -> 183 us (0.84)
  waiting for transfers between devices: 113 us -> 67.9 us
  blocking collectives: 62.6 us -> 72.9 us
    psum x1 -> x0, waiting for transfers between devices: 42.1 us -> none  [shards(): doc_total = lax.psum(feature_block, 'segment')]
    all_gather x0 -> x1, blocking collectives: none -> 10.3 us  [shards(): doc_total = jnp.sum(lax.all_gather(feature_block, 'segment'), axis=0)]
    unnamed x4 -> x3, waiting for transfers between devices: 55.5 us -> 53.1 us
  transfers between devices with their start and end apart: 3 -> 2, of which waited for: 3 -> 2; matrix products, arithmetic and copies ran while one was open for 1% -> 1% of each run, Pallas kernels for 0% -> 0%
where the time goes in v1:
time: 183 us
  blocking collectives  72.9 us (40%)
  waiting for transfers between devices  67.9 us (37%)
  matrix products  21.3 us (12%)
  between operations  14.8 us (8%)
  other arithmetic  4.61 us (3%)
    unnamed x3, waiting for transfers between devices  53.1 us
    unnamed x1, blocking collectives  18.3 us
    psum x1, blocking collectives, shards(): combined = lax.psum(head_terms, 'segment')  16.2 us
    reduce_scatter x1, waiting for transfers between devices, shards(): lax.psum_scatter(section_part, 'seq', scatter_dimension=1, tiled=True)  14.7 us
    all_gather x1, blocking collectives, shards(): lax.all_gather(keys_here, 'seq', axis=0, tiled=True)  14.1 us
    all_gather x1, blocking collectives, shards(): lax.all_gather(values_here, 'seq', axis=0, tiled=True)  14.1 us
    all_gather x1, blocking collectives, shards(): doc_total = jnp.sum(lax.all_gather(feature_block, 'segment'), axis=0)  10.3 us
    dot_general x1, matrix products, shards(): partial_value = jnp.dot(member, tokens, preferred_element_type=jnp.float32)  8.85 us
  transfers between devices with their start and end apart: 2, of which 2 were waited for; matrix products, arithmetic and copies ran while one was open for 1% of the time, Pallas kernels for 0%

profile of v1, /device:TPU:0, one launch (start us, length us, event | category | flops | bytes accessed | tf_op | source)
XLA Modules:
  0.0 182.6 jit_solution(13610954959947405859)
XLA Ops:
  6.5 0.0 copy-start
  6.5 0.0 reduce-scatter.2.cloned.1.call-start
  6.5 0.9 fusion.30
  7.4 0.1 copy.25
  7.5 0.1 reduce-window.7
  7.6 0.1 reduce
  7.7 0.7 bitcast_subtract_fusion
  8.4 8.8 %fusion.3 = f32[64,8192]{1,0:T(8,128)S(1)} fusion(bf16[1,1024,8192]{2,1,0:T(8,128)(2,1)} %param.10, f32[64]{0:T(128)S(1)} %get-tuple-element.6, s32[1024]{0:T(1024)S(1)} %iota_add_fusion, s32[64]{0:T(128)S(1)} %reduce, s32[64]{0:T(128)S(1)} %bitcast_subtract_fusion), kind=kOutput, calls=%fused_computation.3 | convolution fusion | flops 1074462720 | bytes 18879232 | tf_op jit(solution)/shard_map/dot_general | solution.py:24
  17.3 0.0 copy-start.2
  17.3 0.0 copy-start.4
  17.3 0.0 copy-start.3
  17.3 1.8 %fusion.25 = f32[32,8192]{1,0:T(8,128)} fusion(f32[64,8192]{1,0:T(8,128)S(1)} %fusion.3, s32[64]{0:T(128)S(1)} %get-tuple-element.9), kind=kOutput, calls=%fused_computation.34 | convolution fusion | flops 201328640 | bytes 3145984 | tf_op jit(solution)/shard_map/dot_general | solution.py:37
  19.1 0.0 reduce-scatter.2.cloned.1.call-update
  19.1 0.0 all-reduce.4.cloned.1.call-start
  19.2 0.0 copy-done.2
  19.2 0.1 eq.52
  19.3 0.0 copy-done.4
  19.3 0.0 copy-done.3
  19.3 0.7 fusion.31
  21.2 0.2 dynamic-update-slice
  21.5 18.3 %all-reduce = bf16[32]{0:T(256)(128)(2,1)S(1)} all-reduce(bf16[32]{0:T(256)(128)(2,1)S(1)} %dynamic-update-slice), channel_id=1, replica_groups=mesh['segment'=4,'seq'=8] {'seq'}, use_global_device_ids=true, to_apply=%add | all-reduce | flops 32 | bytes 128
  39.7 0.1 convert_reduce_fusion
  39.9 14.7 %reduce-scatter.2.cloned.1.call-done = f32[32,1024]{1,0:T(8,128)} async-done(((f32[32,8192]{1,0:T(8,128)}), f32[32,1024]{1,0:T(8,128)}) %reduce-scatter.2.cloned.1.call-update) | async-done | bytes 131088 | tf_op jit(solution)/shard_map/reduce_scatter | solution.py:38
  54.6 10.3 %all-gather = f32[128,1024]{1,0:T(8,128)S(1)} all-gather(f32[32,1024]{1,0:T(8,128)} %reduce-scatter.2.cloned.1.call-done), channel_id=2, replica_groups=mesh['segment'=4,'seq'=8] {'segment'}, dimensions={0}, use_global_device_ids=true | all-gather | bytes 655360 | tf_op jit(solution)/shard_map/all_gather | solution.py:39
  64.9 0.0 copy-start.1
  64.9 3.8 %fusion.20 = f32[32,2048]{1,0:T(8,128)} fusion(bf16[1024,2048]{1,0:T(8,128)(2,1)} %param.14, f32[32,1024]{1,0:T(8,128)S(1)} %reduce_sum.36, f32[32]{0:T(128)S(1)} %broadcast_maximum_fusion), kind=kOutput, calls=%fused_computation.24 | convolution fusion | flops 134283264 | bytes 4587648 | tf_op jit(solution)/shard_map/dot_general | solution.py:41
  68.7 0.0 all-reduce.4.cloned.1.call-update
  68.7 0.1 fusion.29
  68.8 53.1 %all-reduce.4.cloned.1.call-done = f32[32,2048]{1,0:T(8,128)} async-done(((f32[32,2048]{1,0:T(8,128)}), f32[32,2048]{1,0:T(8,128)}) %all-reduce.4.cloned.1.call-update) | async-done | bytes 262160
  121.9 1.0 multiply_reduce_fusion
  122.9 0.0 copy-done.1
  122.9 2.0 %fusion.11 = bf16[1,4,512]{2,1,0:T(4,128)(2,1)S(1)} fusion(bf16[2048,512]{1,0:T(8,128)(2,1)} %param.17, f32[32,2048]{1,0:T(8,128)} %all-reduce.4.cloned.1.call-done, u32[]{:T(128)S(6)} %multiply.11, f32[2048]{0:T(1024)S(1)} %copy-done.1, f32[4]{0:T(128)S(1)} %add_rsqrt_fusion), kind=kOutput, calls=%fused_computation.14 | convolution fusion | flops 8415232 | bytes 2142228 | tf_op jit(solution)/shard_map/dot_general | solution.py:46
  125.0 14.1 %all-gather.2 = bf16[8,4,512]{2,1,0:T(4,128)(2,1)S(1)} all-gather(bf16[1,4,512]{2,1,0:T(4,128)(2,1)S(1)} %fusion.11), channel_id=1, replica_groups=mesh['segment'=4,'seq'=8] {'seq'}, dimensions={0}, use_global_device_ids=true | all-gather | bytes 36864 | tf_op jit(solution)/shard_map/all_gather | solution.py:50
  139.1 2.2 %fusion.8 = f32[4,4,32]{2,1,0:T(4,128)S(1)} fusion(bf16[2048,512]{1,0:T(8,128)(2,1)} %param.16, bf16[32,4,128]{2,1,0:T(4,128)(2,1)S(1)} %reshape.108, pred[4,32]{1,0:T(4,128)(4,1)S(1)} %fusion.29, f32[32,2048]{1,0:T(8,128)} %all-reduce.4.cloned.1.call-done, u32[]{:T(128)S(6)} %multiply.11, f32[2048]{0:T(1024)S(1)} %copy-done.1, f32[4]{0:T(128)S(1)} %add_rsqrt_fusion), kind=kOutput, calls=%fused_computation.7 | convolution fusion | flops 8547328 | bytes 2173076 | tf_op jit(solution)/shard_map/qhd,khd->hqk/dot_general | solution.py:58
  141.2 0.2 fusion.32
  141.4 2.1 %fusion.9 = bf16[1,4,512]{2,1,0:T(4,128)(2,1)S(1)} fusion(bf16[2048,512]{1,0:T(8,128)(2,1)} %param.18, f32[32,2048]{1,0:T(8,128)} %all-reduce.4.cloned.1.call-done, u32[]{:T(128)S(6)} %multiply.11, f32[2048]{0:T(1024)S(1)} %copy-done.1, f32[4]{0:T(128)S(1)} %add_rsqrt_fusion), kind=kOutput, calls=%fused_computation.12 | convolution fusion | flops 8415232 | bytes 2142228 | tf_op jit(solution)/shard_map/dot_general | solution.py:47
  143.5 14.1 %all-gather.1 = bf16[8,4,512]{2,1,0:T(4,128)(2,1)S(1)} all-gather(bf16[1,4,512]{2,1,0:T(4,128)(2,1)S(1)} %fusion.9), channel_id=1, replica_groups=mesh['segment'=4,'seq'=8] {'seq'}, dimensions={0}, use_global_device_ids=true | all-gather | bytes 36864 | tf_op jit(solution)/shard_map/all_gather | solution.py:51
  157.6 0.0 copy-done
  157.6 0.5 fusion.13
  158.1 16.2 %psum.7 = f32[4,2048]{1,0:T(4,128)S(1)} all-reduce(f32[4,2048]{1,0:T(4,128)S(1)} %fusion.13), channel_id=1, replica_groups=mesh['segment'=4,'seq'=8] {'segment'}, use_global_device_ids=true, to_apply=%region_8.9 | all-reduce | flops 8192 | bytes 65536 | tf_op jit(solution)/shard_map/psum | solution.py:68
  174.3 1.5 add_convert_fusion
  (10 shorter events, 0.1 us)
Async XLA Ops:
  6.5 151.0 %copy-start = (bf16[512,2048]{1,0:T(8,128)(2,1)S(1)}, bf16[512,2048]{1,0:T(8,128)(2,1)}, u32[]{:S(2)}) copy-start(bf16[512,2048]{1,0:T(8,128)(2,1)} %param.19) | copy-start | bytes 6291460
  6.5 48.1 %reduce-scatter.2.cloned.1.call-start = ((), (), s32[]{:S(2)}) async-start(), calls=%async_computation.1 | async-start | bytes 1179648 | tf_op jit(solution)/shard_map/reduce_scatter | solution.py:38
  17.3 1.9 %copy-start.2 = (s32[4,64]{1,0:T(4,128)S(1)}, s32[4,64]{1,0:T(4,128)}, u32[]{:S(2)}) copy-start(s32[4,64]{1,0:T(4,128)} %param.12) | copy-start | bytes 3076
  17.3 2.0 %copy-start.4 = (s32[4]{0:T(128)S(1)}, s32[4]{0:T(128)}, u32[]{:S(2)}) copy-start(s32[4]{0:T(128)} %param.13) | copy-start | bytes 52
  17.3 2.0 %copy-start.3 = (u32[32]{0:T(128)S(1)}, u32[32]{0:T(128)}, u32[]{:S(2)}) copy-start(u32[32]{0:T(128)} %constant.45) | copy-start | bytes 388
  19.1 102.8 %all-reduce.4.cloned.1.call-start = ((), (), s32[]{:S(2)}) async-start(), calls=%async_computation.2 | async-start | bytes 524288
  64.9 58.0 %copy-start.1 = (f32[2048]{0:T(1024)S(1)}, f32[2048]{0:T(1024)}, u32[]{:S(2)}) copy-start(f32[2048]{0:T(1024)} %param.15) | copy-start | bytes 24580
Sparse Core Ops, SparseCore 0:
  19.3 35.2 reduce-scatter.1
  68.9 53.0 all-reduce.3
